TPU v7x, 512 devices: a whole 4x4x16 slice. The times are simulated.
512 devices in a mesh: wide: 64 (over y_lo, z, core), narrow: 8 (over x, y_hi).
Axes of the slice: x: 4, y: 4 (y_hi: 2, y_lo: 2; y = y_hi * 2 + y_lo), z: 16, core: 2. Of those that a mesh axis runs over, the one named last changes fastest.
Arguments:
- cell_rows: bfloat16 [32768, 2048], P('wide', 'narrow'), may hold values from -3 to 3
- attn_gain: float32 [2048], replicated, may hold values from 0.1 to 1.9
- ffn_gain: float32 [2048], replicated, may hold values from 0.1 to 1.9
- panels: bfloat16 [64, 2048, 4096], P('wide', None, 'narrow'), may hold values from -0.125 to 0.125
- panel_slot: int32 [64], replicated, may hold values from 0 to 63, each once
- layout: int32 [256, 3], P('wide'), may hold values from 0 to 31, as said below
Outputs:
- encoded: bfloat16 [32768, 2048], P('wide', 'narrow')
Inputs may be any that keep to these rules, and one draw needn't show every extreme that they name: `panel_slot`: the first three entries name the indices of wide that hold this layer's attention panel, feed-forward input panel and feed-forward output panel; all entries differ. `layout`: row b lists the position p(b) of block b itself first, then two other positions of the same netlist at most 2 away; the three differ. One of the two lies before p(b) and one after it, except for the first two and last two positions of a netlist.
All inputs are finite; a program needn't handle non-finite values.
Results may differ from a plain program's by a relative error of at most 0.018.
Values may be sent and summed in bfloat16 or wider, within the bound.
A program may use at most 64 MiB of HBM per device.

v0:
```python
import jax
import jax.numpy as jnp
from jax import lax
from jax.sharding import PartitionSpec as P

HD = 128
BLK = 128
NET_BLOCKS = 32
epsilon = 1e-05


def spread(block, axis, source):
    block = jnp.where(lax.axis_index(axis) == source, block, jnp.zeros_like(block))
    return lax.psum(block, axis)


def extended(shard, sides, width):
    for axis, dim in sides:
        size, length = (lax.axis_size(axis), shard.shape[dim])
        up = [(i, (i + 1) % size) for i in range(size - 1)]
        down = [(j, i) for i, j in up]
        last = lax.slice_in_dim(shard, length - width, length, axis=dim)
        first = lax.slice_in_dim(shard, 0, width, axis=dim)
        before = lax.ppermute(last, axis, up)
        after = lax.ppermute(first, axis, down)
        shard = jnp.concatenate([before, shard, after], axis=dim)
    return shard


def rms_scale(values, gain):
    mean_square = jnp.mean(values * values, axis=-1, keepdims=True)
    return values * lax.rsqrt(mean_square + epsilon) * gain


def block_mask(layout, query_index):
    wanted = query_index[:, None] + jnp.arange(5, dtype=jnp.int32)[None, :] - 2
    return jnp.any(layout[:, :, None] == wanted[:, None, :], axis=1)


def on_device(cell_rows, attn_gain, ffn_gain, panels, panel_slot, layout):
    attn_panel = spread(panels[0], "wide", panel_slot[0])
    row_count = cell_rows.shape[0]
    block_count = row_count // BLK
    cell_full = lax.all_gather(cell_rows, "narrow", axis=1, tiled=True)
    normed = rms_scale(cell_full.astype(jnp.float32), attn_gain).astype(jnp.bfloat16)
    model_width = attn_panel.shape[0]
    head_count = attn_panel.shape[1] // (4 * HD)
    attn_table = attn_panel.reshape(model_width, head_count, 4, HD)
    projected = jnp.einsum(
        "td,dhjc->thjc", normed, attn_table[:, :, :3, :], preferred_element_type=jnp.float32
    ).astype(jnp.bfloat16)
    key_values = projected[:, :, 1:, :].reshape(row_count, head_count * 2 * HD)
    key_window = extended(key_values, (("wide", 0),), 2 * BLK)
    pair_blocks = key_window.reshape(block_count + 4, BLK, head_count, 2, HD)
    stacked = jnp.stack([pair_blocks[offset : offset + block_count] for offset in range(5)], axis=1)
    query_index = (
        lax.axis_index("wide") * block_count
        + jnp.arange(block_count, dtype=jnp.int32)
        + block_count // 2
    ) % NET_BLOCKS
    allowed = block_mask(layout, query_index)
    queries = projected[:, :, 0, :].reshape(block_count, BLK, head_count, HD)
    scores = jnp.einsum(
        "bqhc,bokhc->bhqok", queries, stacked[:, :, :, :, 0, :], preferred_element_type=jnp.float32
    ) * HD ** (-0.5)
    lifted = jnp.where(allowed[:, None, None, :, None], jnp.exp(scores), jnp.float32(0.0))
    weights = (lifted / jnp.sum(lifted, axis=(3, 4), keepdims=True)).astype(jnp.bfloat16)
    head_out = jnp.einsum(
        "bhqok,bokhc->bqhc", weights, stacked[:, :, :, :, 1, :], preferred_element_type=jnp.float32
    ).astype(jnp.bfloat16)
    head_out = head_out.reshape(row_count, head_count * HD)
    out_rows = attn_table[:, :, 3, :].reshape(model_width, head_count * HD)
    partial_value = lax.dot_general(
        head_out, out_rows, (((1,), (1,)), ((), ())), preferred_element_type=jnp.float32
    )
    attn_part = lax.psum_scatter(
        partial_value.astype(jnp.bfloat16), "narrow", scatter_dimension=1, tiled=True
    ).astype(jnp.float32)
    stream = (cell_rows.astype(jnp.float32) + attn_part).astype(jnp.bfloat16)
    stream_full = lax.all_gather(stream, "narrow", axis=1, tiled=True)
    up_panel = spread(panels[0], "wide", panel_slot[1])
    down_panel = spread(panels[0], "wide", panel_slot[2])
    normed_ffn = rms_scale(stream_full.astype(jnp.float32), ffn_gain).astype(jnp.bfloat16)
    hidden = jax.nn.gelu(
        jnp.dot(normed_ffn, up_panel, preferred_element_type=jnp.float32), approximate=False
    ).astype(jnp.bfloat16)
    ffn_part = lax.dot_general(
        hidden, down_panel, (((1,), (1,)), ((), ())), preferred_element_type=jnp.float32
    )
    mixed_units = lax.psum_scatter(
        ffn_part.astype(jnp.bfloat16), "narrow", scatter_dimension=1, tiled=True
    ).astype(jnp.float32)
    return (stream.astype(jnp.float32) + mixed_units).astype(jnp.bfloat16)


def solution(mesh):
    return jax.shard_map(
        on_device,
        mesh=mesh,
        in_specs=(P("wide", "narrow"), P(), P(), P("wide", None, "narrow"), P(), P("wide", None)),
        out_specs=P("wide", "narrow"),
        check_vma=False,
    )
```

profile of v0, /device:TPU:32, one launch (start us, length us, event | category | flops | bytes accessed | tf_op | source)
XLA Modules:
  0.0 769.4 jit_solution(15220941853354655202)
XLA Ops:
  7.4 0.0 all-gather.3.cloned.1.call-start
  7.4 0.7 all-gather.3.cloned.1.call-update
  8.1 0.0 all-reduce.3.cloned.1.call-start
  8.1 1.4 fusion.95
  11.5 4.0 broadcast_select_fusion
  15.4 2.4 copy.23
  17.8 0.0 all-reduce.3.cloned.1.call-update
  17.9 0.0 reduce-scatter.3.cloned.1.call-start
  17.9 69.8 %all-gather.3.cloned.1.call-done = bf16[512,2048]{1,0:T(8,128)(2,1)} async-done(((bf16[512,256]{1,0:T(8,128)(2,1)}), bf16[512,2048]{1,0:T(8,128)(2,1)}) %all-gather.3.cloned.1.call-update) | async-done | bytes 2097168 | tf_op jit(solution)/shard_map/all_gather | solution.py:44
  87.7 2.1 fusion
  89.8 0.0 copy-start.1
  89.8 0.0 copy-start.6
  89.8 386.0 %all-reduce.3.cloned.1.call-done = (bf16[2048,512]{1,0:T(8,128)(2,1)}, bf16[2048,512]{1,0:T(8,128)(2,1)}, bf16[2048,1,4,128]{0,3,2,1:T(8,128)(2,1)}) async-done(((bf16[2048,512]{1,0:T(8,128)(2,1)}, bf16[2048,512]{1,0:T(8,128)(2,1)}, bf16[2048,1,4,128]{0,3,2,1:T(8,128)(2,1)}), (bf16[2048,512]{1,0:T(8,128)(2,1)}, bf16[2048,512]{1,0:T(8,128)(2,1)}, ...) | async-done | bytes 6291472 | tf_op jit(solution)/shard_map/psum | solution.py:14
  475.8 1.5 slice.80
  477.3 0.0 copy-done.1
  477.3 0.0 copy-done.6
  477.3 1.1 fusion.8
  478.4 0.0 copy-start.5
  478.4 0.1 convert_bitcast_fusion
  478.5 0.1 copy.24
  478.6 1.9 collective-permute-start
  480.5 0.1 copy.26
  480.6 3.6 collective-permute-start.1
  484.3 0.1 add_add_fusion
  484.4 0.0 copy-done.5
  484.4 0.1 copy.33
  484.5 0.1 compare_reduce_fusion
  484.6 0.2 copy.39
  484.8 0.1 copy.25
  484.9 0.1 copy.40
  485.0 0.0 collective-permute-done
  485.0 1.8 collective-permute-done.1
  486.8 0.1 pad_maximum_fusion
  486.9 0.1 stack.18
  486.9 0.7 copy_dynamic-update-slice_fusion.3
  487.7 0.1 stack.19
  487.7 0.1 stack.21
  487.8 0.1 stack.22
  487.9 0.7 copy_dynamic-update-slice_fusion.2
  488.6 0.8 constant_dynamic-update-slice_fusion
  489.4 0.7 copy_dynamic-update-slice_fusion.1
  490.1 0.7 copy_dynamic-update-slice_fusion
  490.9 1.6 fusion.96
  492.5 0.0 copy-done.4
  492.5 0.4 fusion.16
  492.9 0.0 copy-start.3
  492.9 3.1 convolution_convert_fusion
  496.0 0.0 reduce-scatter.3.cloned.1.call-update
  496.1 0.0 copy-start.7
  496.1 0.0 all-gather.5.cloned.1.call-start
  496.1 88.7 %reduce-scatter.3.cloned.1.call-done = bf16[512,256]{1,0:T(8,128)(2,1)} async-done(((bf16[512,2048]{1,0:T(8,128)(2,1)}), bf16[512,256]{1,0:T(8,128)(2,1)}) %reduce-scatter.3.cloned.1.call-update) | async-done | bytes 262160 | tf_op jit(solution)/shard_map/reduce_scatter | solution.py:76
  584.8 0.0 copy-done.3
  584.8 1.7 add_convert_fusion.1
  586.5 0.0 all-gather.5.cloned.1.call-update
  586.5 0.0 reduce-scatter.5.cloned.1.call-start
  586.6 72.5 %all-gather.5.cloned.1.call-done = bf16[512,2048]{1,0:T(8,128)(2,1)} async-done(((bf16[512,256]{1,0:T(8,128)(2,1)}), bf16[512,2048]{1,0:T(8,128)(2,1)}) %all-gather.5.cloned.1.call-update) | async-done | bytes 2097168 | tf_op jit(solution)/shard_map/all_gather | solution.py:80
  659.1 2.2 fusion.3
  661.3 0.0 copy-done.7
  661.4 0.0 copy-done.2
  661.4 8.1 %convolution_convert_fusion.1 = bf16[512,2048]{1,0:T(8,128)(2,1)} fusion(bf16[2048,512]{1,0:T(8,128)(2,1)} %get-tuple-element.5, bf16[2048,512]{1,0:T(8,128)(2,1)} %get-tuple-element.6, bf16[512,2048]{1,0:T(8,128)(2,1)S(1)} %copy-done.2, f32[2048]{0:T(1024)S(1)} %copy-done.7, f32[512]{0:T(512)S(1)} %add_rsqrt_fusion), kind=kOutput, calls=%fused_computation.11 | convolution fusion | flops 2169765888 | bytes 8398848 | tf_op jit(solution)/shard_map/dot_general | solution.py:87
  669.5 0.0 reduce-scatter.5.cloned.1.call-update
  669.5 91.0 %reduce-scatter.5.cloned.1.call-done = bf16[512,256]{1,0:T(8,128)(2,1)} async-done(((bf16[512,2048]{1,0:T(8,128)(2,1)}), bf16[512,256]{1,0:T(8,128)(2,1)}) %reduce-scatter.5.cloned.1.call-update) | async-done | bytes 262160 | tf_op jit(solution)/shard_map/reduce_scatter | solution.py:90
  760.5 0.0 copy-done
  760.5 1.7 add_convert_fusion
  (9 shorter events, 0.1 us)
Async XLA Ops:
  7.4 80.3 %all-gather.3.cloned.1.call-start = ((), (), s32[]{:S(2)}) async-start(), calls=%async_computation.2 | async-start | bytes 2359296 | tf_op jit(solution)/shard_map/all_gather | solution.py:44
  8.1 467.7 %all-reduce.3.cloned.1.call-start = ((), (), s32[]{:S(2)}) async-start(), calls=%async_computation.6 | async-start | bytes 12582912 | tf_op jit(solution)/shard_map/psum | solution.py:14
  17.9 566.9 %reduce-scatter.3.cloned.1.call-start = ((), (), s32[]{:S(2)}) async-start(), calls=%async_computation.3 | async-start | bytes 2359296 | tf_op jit(solution)/shard_map/reduce_scatter | solution.py:76
  89.8 387.5 %copy-start.1 = (bf16[512,2048]{1,0:T(8,128)(2,1)S(1)}, bf16[512,2048]{1,0:T(8,128)(2,1)}, u32[]{:S(2)}) copy-start(bf16[512,2048]{1,0:T(8,128)(2,1)} %all-gather.3.cloned.1.call-done) | copy-start | bytes 6291460
  89.8 387.5 %copy-start.6 = (f32[2048]{0:T(1024)S(1)}, f32[2048]{0:T(1024)}, u32[]{:S(2)}) copy-start(f32[2048]{0:T(1024)} %param.7) | copy-start | bytes 24580
  478.4 6.0 copy-start.5
  478.6 6.4 collective-permute-start
  480.6 6.1 collective-permute-start.1
  490.9 1.6 copy-start.4
  492.9 91.9 %copy-start.3 = (bf16[512,256]{1,0:T(8,128)(2,1)S(1)}, bf16[512,256]{1,0:T(8,128)(2,1)}, u32[]{:S(2)}) copy-start(bf16[512,256]{1,0:T(8,128)(2,1)} %param.6) | copy-start | bytes 786436
  496.1 165.3 %copy-start.7 = (f32[2048]{0:T(1024)S(1)}, f32[2048]{0:T(1024)}, u32[]{:S(2)}) copy-start(f32[2048]{0:T(1024)} %param.8) | copy-start | bytes 24580
  496.1 163.0 %all-gather.5.cloned.1.call-start = ((), (), s32[]{:S(2)}) async-start(), calls=%async_computation.4 | async-start | bytes 2359296 | tf_op jit(solution)/shard_map/all_gather | solution.py:80
  586.5 174.0 %reduce-scatter.5.cloned.1.call-start = ((), (), s32[]{:S(2)}) async-start(), calls=%async_computation.5 | async-start | bytes 2359296 | tf_op jit(solution)/shard_map/reduce_scatter | solution.py:90
  659.1 2.2 copy-start.2
  669.5 91.1 %copy-start = (bf16[512,256]{1,0:T(8,128)(2,1)S(1)}, bf16[512,256]{1,0:T(8,128)(2,1)}, u32[]{:S(2)}) copy-start(bf16[512,256]{1,0:T(8,128)(2,1)} %add_convert_fusion.1) | copy-start | bytes 786436
Sparse Core Ops, SparseCore 0:
  11.2 76.4 all-gather.2
  496.2 88.5 reduce-scatter.2
  587.9 71.1 all-gather.4
  669.6 90.8 reduce-scatter.4
Sparse Core Ops, SparseCore 1:
  18.0 457.7 all-reduce.2
where the time goes:
time: 770 us; the launch traced here: 769 us
  waiting for transfers between devices  710 us (92%)
  between operations  16.7 us (2%)
  matrix products  14.3 us (2%)
  other arithmetic  12 us (2%)
  local copies, waits for them, and re-layouts  10.1 us (1%)
    psum x1, waiting for transfers between devices, spread(): return lax.psum(block, axis)  386 us
    reduce_scatter x1, waiting for transfers between devices, on_device(): lax.psum_scatter(ffn_part.astype(jnp.bfloat16), 'narrow', scatter_dimensi...  91 us
    reduce_scatter x1, waiting for transfers between devices, on_device(): lax.psum_scatter(partial_value.astype(jnp.bfloat16), 'narrow', scatter_di...  88.7 us
    all_gather x1, waiting for transfers between devices, on_device(): stream_full = lax.all_gather(stream, 'narrow', axis=1, tiled=True)  72.5 us
    all_gather x1, waiting for transfers between devices, on_device(): cell_full = lax.all_gather(cell_rows, 'narrow', axis=1, tiled=True)  69.8 us
  transfers between devices with their start and end apart: 7, of which 6 were waited for; matrix products, arithmetic and copies ran while one was open for 1% of the time, Pallas kernels for 0%

commit v1 on v0

--- a/solution.py
+++ b/solution.py
@@ -77,7 +77,9 @@
         partial_value.astype(jnp.bfloat16), "narrow", scatter_dimension=1, tiled=True
     ).astype(jnp.float32)
     stream = (cell_rows.astype(jnp.float32) + attn_part).astype(jnp.bfloat16)
-    stream_full = lax.all_gather(stream, "narrow", axis=1, tiled=True)
+    stream_full = jnp.concatenate(
+        lax.all_to_all(jnp.stack([stream] * lax.axis_size("narrow")), "narrow", 0, 0), axis=1
+    )
     up_panel = spread(panels[0], "wide", panel_slot[1])
     down_panel = spread(panels[0], "wide", panel_slot[2])
     normed_ffn = rms_scale(stream_full.astype(jnp.float32), ffn_gain).astype(jnp.bfloat16)

time: 770 us -> 721 us (0.936)
  waiting for transfers between devices: 710 us -> 638 us
  blocking collectives: 0 us -> 30 us
    all_gather x1 -> x0, waiting for transfers between devices: 72.5 us -> none  [on_device(): stream_full = lax.all_gather(stream, 'narrow', axis=1, tiled=True)]
    all_to_all x0 -> x1, blocking collectives: none -> 30 us  [on_device(): lax.all_to_all(jnp.stack([stream] * lax.axis_size('narrow')), 'narrow', 0...]
  transfers between devices with their start and end apart: 7 -> 6, of which waited for: 6 -> 5; matrix products, arithmetic and copies ran while one was open for 1% -> 1% of each run, Pallas kernels for 0% -> 0%
where the time goes in v1:
time: 721 us
  waiting for transfers between devices  638 us (88%)
  blocking collectives  30 us (4%)
  between operations  16.7 us (2%)
  matrix products  13.1 us (2%)
  other arithmetic  10.1 us (1%)
    psum x1, waiting for transfers between devices, spread(): return lax.psum(block, axis)  386 us
    reduce_scatter x1, waiting for transfers between devices, on_device(): lax.psum_scatter(ffn_part.astype(jnp.bfloat16), 'narrow', scatter_dimensi...  90.7 us
    reduce_scatter x1, waiting for transfers between devices, on_device(): lax.psum_scatter(partial_value.astype(jnp.bfloat16), 'narrow', scatter_di...  88.7 us
    all_gather x1, waiting for transfers between devices, on_device(): cell_full = lax.all_gather(cell_rows, 'narrow', axis=1, tiled=True)  69.7 us
    all_to_all x1, blocking collectives, on_device(): lax.all_to_all(jnp.stack([stream] * lax.axis_size('narrow')), 'narrow', 0...  30 us
  transfers between devices with their start and end apart: 6, of which 5 were waited for; matrix products, arithmetic and copies ran while one was open for 1% of the time, Pallas kernels for 0%

profile of v1, /device:TPU:32, one launch (start us, length us, event | category | flops | bytes accessed | tf_op | source)
XLA Modules:
  0.0 720.6 jit_solution(12930152803515390527)
XLA Ops:
  7.4 0.0 all-gather.2.cloned.1.call-start
  7.4 0.7 all-gather.2.cloned.1.call-update
  8.1 0.0 all-reduce.3.cloned.1.call-start
  8.1 1.4 fusion.87
  11.5 4.0 select_bitcast_fusion.1
  15.4 2.4 copy.24
  17.9 0.0 all-reduce.3.cloned.1.call-update
  17.9 0.0 reduce-scatter.3.cloned.1.call-start
  17.9 69.7 %all-gather.2.cloned.1.call-done = bf16[512,2048]{1,0:T(8,128)(2,1)} async-done(((bf16[512,256]{1,0:T(8,128)(2,1)}), bf16[512,2048]{1,0:T(8,128)(2,1)}) %all-gather.2.cloned.1.call-update) | async-done | bytes 2097168 | tf_op jit(solution)/shard_map/all_gather | solution.py:44
  87.7 2.1 fusion
  89.8 0.0 copy-start
  89.8 0.0 copy-start.4
  89.8 386.0 %all-reduce.3.cloned.1.call-done = (bf16[2048,512]{1,0:T(8,128)(2,1)}, bf16[2048,1,4,128]{0,3,2,1:T(8,128)(2,1)}, bf16[2048,512]{1,0:T(8,128)(2,1)}) async-done(((bf16[2048,512]{1,0:T(8,128)(2,1)}, bf16[2048,1,4,128]{0,3,2,1:T(8,128)(2,1)}, bf16[2048,512]{1,0:T(8,128)(2,1)}), (bf16[2048,512]{1,0:T(8,128)(2,1)}, bf16[2048,1,4,128]{0,3,2,1:T(8,128)(2,1)}, ...) | async-done | bytes 6291472 | tf_op jit(solution)/shard_map/psum | solution.py:14
  475.8 1.5 slice.80
  477.3 0.0 copy-done
  477.3 0.0 copy-done.4
  477.3 1.1 fusion.5
  478.4 0.0 copy-start.3
  478.4 0.1 convert_bitcast_fusion
  478.5 0.1 copy.25
  478.6 1.9 collective-permute-start
  480.5 0.1 copy.27
  480.6 3.6 collective-permute-start.1
  484.3 0.1 add_add_fusion
  484.4 0.0 copy-done.3
  484.4 0.1 copy.34
  484.5 0.1 compare_reduce_fusion
  484.6 0.2 copy.41
  484.8 0.1 copy.26
  484.9 0.1 copy.42
  485.0 0.0 collective-permute-done
  485.0 1.8 collective-permute-done.1
  486.8 0.1 pad_maximum_fusion
  486.9 0.1 stack.14
  487.0 0.1 stack.30
  487.1 0.1 stack.32
  487.1 0.1 stack.33
  487.2 0.1 copy_dynamic-update-slice_fusion.2
  487.3 0.1 copy_dynamic-update-slice_fusion.1
  487.4 0.1 copy_dynamic-update-slice_fusion
  487.5 0.4 fusion.88
  487.9 0.4 fusion.11
  488.3 0.0 copy-start.1
  488.3 3.1 convolution_convert_fusion
  491.5 0.0 reduce-scatter.3.cloned.1.call-update
  491.5 0.0 reduce-scatter.5.cloned.1.call-start
  491.5 88.7 %reduce-scatter.3.cloned.1.call-done = bf16[512,256]{1,0:T(8,128)(2,1)} async-done(((bf16[512,2048]{1,0:T(8,128)(2,1)}), bf16[512,256]{1,0:T(8,128)(2,1)}) %reduce-scatter.3.cloned.1.call-update) | async-done | bytes 262160 | tf_op jit(solution)/shard_map/reduce_scatter | solution.py:76
  580.2 0.0 copy-done.1
  580.2 1.0 add_convert_fusion.1
  581.3 0.1 copy.37
  581.4 0.2 stack.35
  581.6 30.0 %all_to_all.5 = bf16[8,512,256]{1,2,0:T(8,128)(2,1)S(1)} all-to-all(bf16[8,512,256]{1,2,0:T(8,128)(2,1)S(1)} %stack.35), channel_id=1, replica_groups=mesh['wide'=64,'narrow'=8] {'narrow'}, dimensions={0} | all-to-all | bytes 4194304 | tf_op jit(solution)/shard_map/all_to_all | solution.py:81
  611.6 0.0 copy-start.2
  611.6 0.5 multiply_reduce_fusion
  612.2 0.2 copy-done.2
  612.3 0.5 fusion.4
  612.9 8.1 %convolution_convert_fusion.1 = bf16[512,2048]{1,0:T(8,128)(2,1)} fusion(bf16[2048,512]{1,0:T(8,128)(2,1)} %get-tuple-element.5, bf16[512,2048]{0,1:T(8,128)(2,1)S(1)} %fusion.4, bf16[2048,512]{1,0:T(8,128)(2,1)} %get-tuple-element.7), kind=kOutput, calls=%fused_computation.10 | convolution fusion | flops 2165571584 | bytes 8388608 | tf_op jit(solution)/shard_map/dot_general | solution.py:89
  621.0 0.0 reduce-scatter.5.cloned.1.call-update
  621.0 90.7 %reduce-scatter.5.cloned.1.call-done = bf16[512,256]{1,0:T(8,128)(2,1)} async-done(((bf16[512,2048]{1,0:T(8,128)(2,1)}), bf16[512,256]{1,0:T(8,128)(2,1)}) %reduce-scatter.5.cloned.1.call-update) | async-done | bytes 262160 | tf_op jit(solution)/shard_map/reduce_scatter | solution.py:92
  711.7 1.7 add_convert_fusion
  (8 shorter events, 0.1 us)
Async XLA Ops:
  7.4 80.3 %all-gather.2.cloned.1.call-start = ((), (), s32[]{:S(2)}) async-start(), calls=%async_computation.3 | async-start | bytes 2359296 | tf_op jit(solution)/shard_map/all_gather | solution.py:44
  8.1 467.7 %all-reduce.3.cloned.1.call-start = ((), (), s32[]{:S(2)}) async-start(), calls=%async_computation.6 | async-start | bytes 12582912 | tf_op jit(solution)/shard_map/psum | solution.py:14
  17.9 562.4 %reduce-scatter.3.cloned.1.call-start = ((), (), s32[]{:S(2)}) async-start(), calls=%async_computation.4 | async-start | bytes 2359296 | tf_op jit(solution)/shard_map/reduce_scatter | solution.py:76
  89.8 387.5 %copy-start = (bf16[512,2048]{1,0:T(8,128)(2,1)S(1)}, bf16[512,2048]{1,0:T(8,128)(2,1)}, u32[]{:S(2)}) copy-start(bf16[512,2048]{1,0:T(8,128)(2,1)} %all-gather.2.cloned.1.call-done) | copy-start | bytes 6291460
  89.8 387.5 %copy-start.4 = (f32[2048]{0:T(1024)S(1)}, f32[2048]{0:T(1024)}, u32[]{:S(2)}) copy-start(f32[2048]{0:T(1024)} %param.7) | copy-start | bytes 24580
  478.4 6.0 copy-start.3
  478.6 6.4 collective-permute-start
  480.6 6.1 collective-permute-start.1
  488.3 91.9 %copy-start.1 = (bf16[512,256]{1,0:T(8,128)(2,1)S(1)}, bf16[512,256]{1,0:T(8,128)(2,1)}, u32[]{:S(2)}) copy-start(bf16[512,256]{1,0:T(8,128)(2,1)} %param.6) | copy-start | bytes 786436
  491.5 220.2 %reduce-scatter.5.cloned.1.call-start = ((), (), s32[]{:S(2)}) async-start(), calls=%async_computation.5 | async-start | bytes 2359296 | tf_op jit(solution)/shard_map/reduce_scatter | solution.py:92
  611.6 0.7 copy-start.2
Sparse Core Ops, SparseCore 0:
  11.2 76.4 all-gather.1
  491.6 88.5 reduce-scatter.2
  621.1 90.5 reduce-scatter.4
Sparse Core Ops, SparseCore 1:
  18.0 457.7 all-reduce.2
